TPU v7x, 32 devices: a whole 2x2x4 slice. The times are simulated.
32 devices in a mesh: groups: 2 (over x), ctx: 16 (over z, y, core).
Axes of the slice: x: 2, y: 2, z: 4, core: 2. Of those that a mesh axis runs over, the one named last changes fastest.
Arguments:
- query_input: bfloat16 [32, 1536], P('groups'), parts along dimension 0, may hold values from -20 to 20
- query_gain: bfloat16 [1536], replicated, may hold values from 0.5 to 1.5
- nope_weight: bfloat16 [1536, 4096], P(None, 'ctx'), may hold values from -0.15625 to 0.15625
- rope_weight: bfloat16 [1536, 2048], P(None, 'ctx'), may hold values from -0.15625 to 0.15625
- key_up: bfloat16 [32, 128, 512], P('ctx'), may hold values from -0.5 to 0.5
- value_up: bfloat16 [32, 512, 128], P('ctx'), may hold values from -1 to 1
- out_weight: bfloat16 [4096, 7168], P('ctx'), may hold values from -0.09375 to 0.09375
- cache_latent: bfloat16 [4, 32768, 512], P('groups', 'ctx'), parts along dimension 0, may hold values from -8 to 8
- cache_rope: bfloat16 [4, 64, 32768], P('groups', None, 'ctx'), parts along dimension 0, may hold values from -256 to 256
- cached_length: int32 [4], P('groups'), parts along dimension 0, may hold values from 16384 to 32760, as said below
Outputs:
- attn_out: bfloat16 [32, 7168], P('groups'), parts along dimension 0
There are 2 independent parts, one for each index of `groups`. A program takes and returns all parts, laid end to end along the dimension named above; an argument that names none is the same for every part. Nothing has to cross between parts.
Inputs may be any that keep to these rules, and one draw needn't show every extreme that they name: `cached_length`: in every part one request has exactly 32760, so that its last new token sees the cache's last position.
All inputs are finite; a program needn't handle non-finite values.
Results may differ from a plain program's by a relative error of at most 0.012.
Values may be sent and summed in bfloat16 or wider, within the bound.
A program may use at most 128 MiB of HBM per device.

v0:
```python
import math
import jax
import jax.numpy as jnp
from jax import lax
from jax.sharding import PartitionSpec as P

mscale_yarn = 1.0 + 0.1 * math.log(40.0)
masked_score = -1e30


def attend_heads(
    latent_query, rope_query, cache_latent, cache_rope, cached_length, positions, softmax_scale
):
    row_count, head_count, latent_width = latent_query.shape
    rope_width = rope_query.shape[2]
    requests = cache_latent.shape[0]
    stretch_rows = row_count // requests
    peak_list, sum_list, pool_list = ([], [], [])
    for request in range(requests):
        flat_latent = latent_query[request * stretch_rows : (request + 1) * stretch_rows].reshape(
            stretch_rows * head_count, latent_width
        )
        flat_rope = rope_query[request * stretch_rows : (request + 1) * stretch_rows].reshape(
            stretch_rows * head_count, rope_width
        )
        scores = jnp.einsum(
            "ql,pl->qp", flat_latent, cache_latent[request], preferred_element_type=jnp.float32
        )
        scores = (
            scores + jnp.dot(flat_rope, cache_rope[request], preferred_element_type=jnp.float32)
        ) * softmax_scale
        last_seen = (
            cached_length[request]
            + jnp.arange(stretch_rows * head_count, dtype=jnp.int32) // head_count
        )
        visible = positions[None, :] <= last_seen[:, None]
        scores = jnp.where(visible, scores, masked_score)
        block_peak = jnp.max(scores, axis=1)
        weights = jnp.where(visible, jnp.exp(scores - block_peak[:, None]), 0.0)
        block_sum = jnp.sum(weights, axis=1)
        block_pool = jnp.dot(
            weights.astype(jnp.bfloat16), cache_latent[request], preferred_element_type=jnp.float32
        )
        peak_list.append(block_peak.reshape(stretch_rows, head_count))
        sum_list.append(block_sum.reshape(stretch_rows, head_count))
        pool_list.append(block_pool.reshape(stretch_rows, head_count, latent_width))
    return (
        jnp.concatenate(peak_list, axis=0),
        jnp.concatenate(sum_list, axis=0),
        jnp.concatenate(pool_list, axis=0),
    )


def project_heads(pooled, weight_sum, value_up, out_weight):
    attended = (pooled / weight_sum[:, :, None]).astype(jnp.bfloat16)
    head_values = jnp.einsum(
        "rhl,hlv->rhv", attended, value_up, preferred_element_type=jnp.float32
    ).astype(jnp.bfloat16)
    return jnp.dot(
        head_values.reshape(head_values.shape[0], -1),
        out_weight,
        preferred_element_type=jnp.float32,
    )


def local(
    query_input,
    query_gain,
    nope_weight,
    rope_weight,
    key_up,
    value_up,
    out_weight,
    cache_latent,
    cache_rope,
    cached_length,
):
    head_local = key_up.shape[0]
    nope_width = key_up.shape[1]
    rope_width = rope_weight.shape[1] // head_local
    row_count = query_input.shape[0]
    key_count = cache_latent.shape[1]
    widened = query_input.astype(jnp.float32)
    normed = (
        widened
        * lax.rsqrt(jnp.mean(widened * widened, axis=-1, keepdims=True) + 1e-06)
        * query_gain.astype(jnp.float32)
    ).astype(jnp.bfloat16)
    query_nope = (
        jnp.dot(normed, nope_weight, preferred_element_type=jnp.float32)
        .astype(jnp.bfloat16)
        .reshape(row_count, head_local, nope_width)
    )
    query_rope = (
        jnp.dot(normed, rope_weight, preferred_element_type=jnp.float32)
        .astype(jnp.bfloat16)
        .reshape(row_count, head_local, rope_width)
    )
    query_latent = jnp.einsum(
        "rhn,hnl->rhl", query_nope, key_up, preferred_element_type=jnp.float32
    ).astype(jnp.bfloat16)
    softmax_scale = mscale_yarn * mscale_yarn / math.sqrt(nope_width + rope_width)
    positions = lax.axis_index("ctx") * key_count + jnp.arange(key_count, dtype=jnp.int32)
    every_latent, every_rope = (
        lax.all_gather(query_latent, "ctx", axis=1, tiled=True),
        lax.all_gather(query_rope, "ctx", axis=1, tiled=True),
    )
    block_peak, block_sum, block_pool = attend_heads(
        every_latent, every_rope, cache_latent, cache_rope, cached_length, positions, softmax_scale
    )
    pooled_in = lax.all_to_all(block_pool[None], "ctx", split_axis=2, concat_axis=0, tiled=True)
    peak_in = lax.all_to_all(block_peak[None], "ctx", split_axis=2, concat_axis=0, tiled=True)
    sum_in = lax.all_to_all(block_sum[None], "ctx", split_axis=2, concat_axis=0, tiled=True)
    row_top = jnp.max(peak_in, axis=0)
    factor = jnp.exp(peak_in - row_top[None])
    pooled = jnp.sum(pooled_in * factor[..., None], axis=0)
    weight_sum = jnp.sum(sum_in * factor, axis=0)
    partial_value = project_heads(pooled, weight_sum, value_up, out_weight)
    return lax.psum(partial_value, "ctx").astype(jnp.bfloat16)


def solution(mesh):
    placed = (
        P("groups", None),
        P(),
        P(None, "ctx"),
        P(None, "ctx"),
        P("ctx", None, None),
        P("ctx", None, None),
        P("ctx", None),
        P("groups", "ctx", None),
        P("groups", None, "ctx"),
        P("groups"),
    )
    return jax.shard_map(
        local, mesh=mesh, in_specs=placed, out_specs=P("groups", None), check_vma=False
    )
```

profile of v0, /device:TPU:0, one launch (start us, length us, event | category | flops | bytes accessed | tf_op | source)
XLA Modules:
  0.0 175.1 jit_solution(12115778293265833145)
XLA Ops:
  0.0 0.0 copy-start
  0.0 0.0 copy-start.4
  0.0 0.0 copy-start.5
  0.0 1.4 fusion.44
  1.4 0.7 convert_element_type.40
  2.1 0.9 fusion.28
  3.1 0.0 copy-done
  3.1 1.1 fusion.21
  4.1 1.1 fusion.20
  5.2 24.6 %all_gather.6 = bf16[16,32,512]{2,0,1:T(8,128)(2,1)S(1)} all-gather(bf16[16,2,512]{2,0,1:T(8,128)(2,1)S(1)} %fusion.20), channel_id=1, replica_groups=mesh['groups'=2,'ctx'=16] {'ctx'}, dimensions={1}, use_global_device_ids=true | all-gather | bytes 557056 | tf_op jit(solution)/shard_map/all_gather | solution.py:105
  29.9 0.1 copy.76
  30.0 0.0 copy-done.4
  30.0 0.0 copy-done.5
  30.0 0.2 convolution_convert_fusion.3
  30.2 0.1 reshape.79
  30.3 17.8 %all_gather.7 = bf16[16,32,64]{2,0,1:T(8,128)(2,1)S(1)} all-gather(bf16[16,2,64]{2,0,1:T(8,128)(2,1)S(1)} %copy.64), channel_id=1, replica_groups=mesh['groups'=2,'ctx'=16] {'ctx'}, dimensions={1}, use_global_device_ids=true | all-gather | bytes 69632 | tf_op jit(solution)/shard_map/all_gather | solution.py:106
  48.1 0.1 copy.75
  48.2 0.0 copy-start.1
  48.2 2.5 %fusion.6 = f32[256,2048]{1,0:T(8,128)S(1)} fusion(bf16[256,512]{1,0:T(8,128)(2,1)S(1)} %bitcast.80, bf16[2,2048,512]{2,1,0:T(8,128)(2,1)} %param.17), kind=kOutput, calls=%fused_computation.10 | convolution fusion | flops 536870912 | bytes 4456448 | tf_op jit(solution)/shard_map/ql,pl->qp/dot_general | solution.py:26
  50.7 0.3 copy-done.1
  51.0 0.0 copy-start.3
  51.0 0.7 fusion.10
  51.8 1.3 broadcast_add_fusion
  53.1 0.0 copy-done.3
  53.1 0.6 fusion.46
  53.8 0.6 fusion.45
  54.4 1.0 fusion.16
  55.5 0.1 reshape.85
  55.5 0.1 reshape.86
  55.6 0.7 copy.72
  56.3 3.5 %all-to-all-start.2 = ((f32[1,16,32]{1,0,2:T(1,128)}), f32[1,16,32]{1,0,2:T(1,128)S(1)}, u32[]{:S(2)}, u32[]{:S(2)}) async-start(f32[1,16,32]{1,0,2:T(1,128)} %copy.72), calls=%async_computation.2 | async-start | bytes 32768 | tf_op jit(solution)/shard_map/all_to_all | solution.py:113
  59.8 0.1 reshape.84
  59.9 0.1 reshape.83
  60.0 0.0 copy-start.2
  60.0 2.4 %fusion.4 = f32[8,32,512]{2,1,0:T(8,128)S(1)} fusion(bf16[8,32,2048]{2,1,0:T(8,128)(2,1)S(1)} %bitcast.79, bf16[2,2048,512]{2,1,0:T(8,128)(2,1)} %param.17), kind=kOutput, calls=%fused_computation.8 | convolution fusion | flops 536870912 | bytes 3670016 | tf_op jit(solution)/shard_map/dot_general | solution.py:41
  62.4 0.4 copy-done.2
  62.8 0.7 fusion.8
  63.5 0.7 copy.70
  64.2 2.1 %all-to-all-done.2 = f32[1,16,32]{1,0,2:T(1,128)S(1)} async-done(((f32[1,16,32]{1,0,2:T(1,128)}), f32[1,16,32]{1,0,2:T(1,128)S(1)}, u32[]{:S(2)}, u32[]{:S(2)}) %all-to-all-start.2) | async-done | bytes 2080 | tf_op jit(solution)/shard_map/all_to_all | solution.py:113
  66.3 3.9 %all-to-all-start.1 = ((f32[1,16,32]{1,0,2:T(1,128)}), f32[1,16,32]{1,0,2:T(1,128)S(1)}, u32[]{:S(2)}, u32[]{:S(2)}) async-start(f32[1,16,32]{1,0,2:T(1,128)} %copy.70), calls=%async_computation.1 | async-start | bytes 32768 | tf_op jit(solution)/shard_map/all_to_all | solution.py:112
  70.2 0.1 maximum_bitcast_fusion
  70.3 1.6 copy.68
  71.9 0.0 copy-start.6
  71.9 4.8 %all-to-all-done.1 = f32[1,16,32]{1,0,2:T(1,128)S(1)} async-done(((f32[1,16,32]{1,0,2:T(1,128)}), f32[1,16,32]{1,0,2:T(1,128)S(1)}, u32[]{:S(2)}, u32[]{:S(2)}) %all-to-all-start.1) | async-done | bytes 2080 | tf_op jit(solution)/shard_map/all_to_all | solution.py:112
  76.7 3.7 %all-to-all-start = ((f32[1,16,32,512]{3,1,0,2:T(8,128)}), f32[1,16,32,512]{3,1,0,2:T(8,128)S(1)}, u32[]{:S(2)}, u32[]{:S(2)}) async-start(f32[1,16,32,512]{3,1,0,2:T(8,128)} %copy.68), calls=%async_computation | async-start | bytes 2097152 | tf_op jit(solution)/shard_map/all_to_all | solution.py:111
  80.4 0.2 copy.71
  80.6 22.6 %all-to-all-done = f32[1,16,32,512]{3,1,0,2:T(8,128)S(1)} async-done(((f32[1,16,32,512]{3,1,0,2:T(8,128)}), f32[1,16,32,512]{3,1,0,2:T(8,128)S(1)}, u32[]{:S(2)}, u32[]{:S(2)}) %all-to-all-start) | async-done | bytes 1048608 | tf_op jit(solution)/shard_map/all_to_all | solution.py:111
  103.2 1.1 fusion.23
  104.3 0.0 copy-done.6
  104.3 0.2 fusion.22
  104.5 2.6 %fusion.36 = f32[16,7168]{1,0:T(8,128)S(1)} fusion(bf16[256,7168]{1,0:T(8,128)(2,1)} %param.16, bf16[2,2,8,128]{3,2,1,0:T(8,128)(2,1)S(1)} %fusion.22), kind=kOutput, calls=%fused_computation.48 | convolution fusion | flops 58720256 | bytes 4136960 | tf_op jit(solution)/shard_map/dot_general | solution.py:59
  107.1 68.0 %all-reduce.1 = bf16[16,7168]{1,0:T(8,128)(2,1)} all-reduce(f32[16,7168]{1,0:T(8,128)S(1)} %fusion.36), channel_id=1, replica_groups=mesh['groups'=2,'ctx'=16] {'ctx'}, use_global_device_ids=true, to_apply=%region_8.9 | all-reduce | flops 114688 | bytes 688128 | tf_op jit(solution)/shard_map/psum | solution.py:119
  (11 shorter events, 0.2 us)
Async XLA Ops:
  0.0 3.1 %copy-start = (bf16[1536,256]{1,0:T(8,128)(2,1)S(1)}, bf16[1536,256]{1,0:T(8,128)(2,1)}, u32[]{:S(2)}) copy-start(bf16[1536,256]{1,0:T(8,128)(2,1)} %param.12) | copy-start | bytes 2359300
  0.0 30.0 %copy-start.4 = (bf16[16,1536]{1,0:T(8,128)(2,1)S(1)}, bf16[16,1536]{1,0:T(8,128)(2,1)}, u32[]{:S(2)}) copy-start(bf16[16,1536]{1,0:T(8,128)(2,1)} %param.10) | copy-start | bytes 147460
  0.0 30.0 %copy-start.5 = (bf16[1536,128]{1,0:T(8,128)(2,1)S(1)}, bf16[1536,128]{1,0:T(8,128)(2,1)}, u32[]{:S(2)}) copy-start(bf16[1536,128]{1,0:T(8,128)(2,1)} %param.13) | copy-start | bytes 1179652
  48.2 2.8 %copy-start.1 = (bf16[2,2048,512]{2,1,0:T(8,128)(2,1)S(1)}, bf16[2,2048,512]{2,1,0:T(8,128)(2,1)}, u32[]{:S(2)}) copy-start(bf16[2,2048,512]{2,1,0:T(8,128)(2,1)} %param.17) | copy-start | bytes 12582916
  51.0 2.1 %copy-start.3 = (bf16[2,64,2048]{2,1,0:T(8,128)(2,1)S(1)}, bf16[2,64,2048]{2,1,0:T(8,128)(2,1)}, u32[]{:S(2)}) copy-start(bf16[2,64,2048]{2,1,0:T(8,128)(2,1)} %param.18) | copy-start | bytes 1572868
  56.3 10.0 %all-to-all-start.2 = ((f32[1,16,32]{1,0,2:T(1,128)}), f32[1,16,32]{1,0,2:T(1,128)S(1)}, u32[]{:S(2)}, u32[]{:S(2)}) async-start(f32[1,16,32]{1,0,2:T(1,128)} %copy.72), calls=%async_computation.2 | async-start | bytes 32768 | tf_op jit(solution)/shard_map/all_to_all | solution.py:113
  60.0 2.8 %copy-start.2 = (bf16[2,2048,512]{2,1,0:T(8,128)(2,1)S(1)}, bf16[2,2048,512]{2,1,0:T(8,128)(2,1)}, u32[]{:S(2)}) copy-start(bf16[2,2048,512]{2,1,0:T(8,128)(2,1)} %param.17) | copy-start | bytes 12582916
  66.3 10.4 %all-to-all-start.1 = ((f32[1,16,32]{1,0,2:T(1,128)}), f32[1,16,32]{1,0,2:T(1,128)S(1)}, u32[]{:S(2)}, u32[]{:S(2)}) async-start(f32[1,16,32]{1,0,2:T(1,128)} %copy.70), calls=%async_computation.1 | async-start | bytes 32768 | tf_op jit(solution)/shard_map/all_to_all | solution.py:112
  71.9 32.4 %copy-start.6 = (bf16[2,512,128]{2,1,0:T(8,128)(2,1)S(1)}, bf16[2,512,128]{2,1,0:T(8,128)(2,1)}, u32[]{:S(2)}) copy-start(bf16[2,512,128]{2,1,0:T(8,128)(2,1)} %param.15) | copy-start | bytes 786436
  76.7 26.5 %all-to-all-start = ((f32[1,16,32,512]{3,1,0,2:T(8,128)}), f32[1,16,32,512]{3,1,0,2:T(8,128)S(1)}, u32[]{:S(2)}, u32[]{:S(2)}) async-start(f32[1,16,32,512]{3,1,0,2:T(8,128)} %copy.68), calls=%async_computation | async-start | bytes 2097152 | tf_op jit(solution)/shard_map/all_to_all | solution.py:111
where the time goes:
time: 176 us; the launch traced here: 175 us
  blocking collectives  110 us (62%)
  waiting for transfers between devices  29.5 us (17%)
  matrix products  12.8 us (7%)
  starting transfers between devices  11 us (6%)
  local copies, waits for them, and re-layouts  5.92 us (3%)
  other arithmetic  5.27 us (3%)
    psum x1, blocking collectives, local(): return lax.psum(partial_value, 'ctx').astype(jnp.bfloat16)  68 us
    all_gather x1, blocking collectives, local(): lax.all_gather(query_latent, 'ctx', axis=1, tiled=True)  24.6 us
    all_to_all x1, waiting for transfers between devices, local(): lax.all_to_all(block_pool[None], 'ctx', split_axis=2, concat_axis=0, tile...  22.6 us
    all_gather x1, blocking collectives, local(): lax.all_gather(query_rope, 'ctx', axis=1, tiled=True)  17.8 us
    all_to_all x1, waiting for transfers between devices, local(): lax.all_to_all(block_peak[None], 'ctx', split_axis=2, concat_axis=0, tile...  4.8 us
    all_to_all x1, starting transfers between devices, local(): lax.all_to_all(block_peak[None], 'ctx', split_axis=2, concat_axis=0, tile...  3.88 us
    all_to_all x1, starting transfers between devices, local(): lax.all_to_all(block_pool[None], 'ctx', split_axis=2, concat_axis=0, tile...  3.65 us
  transfers between devices with their start and end apart: 3, of which 3 were waited for; matrix products, arithmetic and copies ran while one was open for 3% of the time, Pallas kernels for 0%

commit v1 on v0

--- a/solution.py
+++ b/solution.py
@@ -6,6 +6,11 @@
 
 mscale_yarn = 1.0 + 0.1 * math.log(40.0)
 masked_score = -1e30
+
+
+def summed_here(value, name):
+    pieces = lax.all_gather(value, name)
+    return jnp.sum(pieces, axis=0)
 
 
 def attend_heads(
@@ -116,7 +121,7 @@
     pooled = jnp.sum(pooled_in * factor[..., None], axis=0)
     weight_sum = jnp.sum(sum_in * factor, axis=0)
     partial_value = project_heads(pooled, weight_sum, value_up, out_weight)
-    return lax.psum(partial_value, "ctx").astype(jnp.bfloat16)
+    return summed_here(partial_value, "ctx").astype(jnp.bfloat16)
 
 
 def solution(mesh):

time: 176 us -> 203 us (1.15)
  waiting for transfers between devices: 29.5 us -> 97.3 us
  blocking collectives: 110 us -> 42.3 us
  between operations: 0.19 us -> 13.6 us
  other arithmetic: 5.27 us -> 12.3 us
  matrix products: 12.8 us -> 18.1 us
  starting transfers between devices: 11 us -> 13.1 us
    all_gather x0 -> x1, waiting for transfers between devices: none -> 69.9 us  [summed_here(): pieces = lax.all_gather(value, name)]
    psum x1 -> x0, blocking collectives: 68 us -> none  [local(): return lax.psum(partial_value, 'ctx').astype(jnp.bfloat16)]
    all_gather x1, blocking collectives: 24.6 us -> 18.9 us  [local(): lax.all_gather(query_latent, 'ctx', axis=1, tiled=True)]
    all_gather x1, blocking collectives: 17.8 us -> 23.5 us  [local(): lax.all_gather(query_rope, 'ctx', axis=1, tiled=True)]
    all_to_all x1, waiting for transfers between devices: 4.8 us -> 0.01 us  [local(): lax.all_to_all(block_peak[None], 'ctx', split_axis=2, concat_axis=0, tile...]
    reduce_sum x0 -> x1, other arithmetic: none -> 4.17 us  [summed_here(): return jnp.sum(pieces, axis=0)]
    reduce_sum x1, other arithmetic: 1.04 us -> 3.83 us  [attend_heads(): block_sum = jnp.sum(weights, axis=1)]
    all_to_all x1, waiting for transfers between devices: 2.1 us -> 4.8 us  [local(): lax.all_to_all(block_sum[None], 'ctx', split_axis=2, concat_axis=0, tiled...]
  transfers between devices with their start and end apart: 3 -> 4, of which waited for: 3 -> 3; matrix products, arithmetic and copies ran while one was open for 3% -> 6% of each run, Pallas kernels for 0% -> 0%
where the time goes in v1:
time: 203 us; the launch traced here: 202 us
  waiting for transfers between devices  97.3 us (48%)
  blocking collectives  42.3 us (21%)
  matrix products  18.1 us (9%)
  between operations  13.6 us (7%)
  starting transfers between devices  13.1 us (6%)
  other arithmetic  12.3 us (6%)
  local copies, waits for them, and re-layouts  5.56 us (3%)
    all_gather x1, waiting for transfers between devices, summed_here(): pieces = lax.all_gather(value, name)  69.9 us
    all_gather x1, blocking collectives, local(): lax.all_gather(query_rope, 'ctx', axis=1, tiled=True)  23.5 us
    all_to_all x1, waiting for transfers between devices, local(): lax.all_to_all(block_pool[None], 'ctx', split_axis=2, concat_axis=0, tile...  22.6 us
    all_gather x1, blocking collectives, local(): lax.all_gather(query_latent, 'ctx', axis=1, tiled=True)  18.9 us
    all_to_all x1, starting transfers between devices, local(): lax.all_to_all(block_sum[None], 'ctx', split_axis=2, concat_axis=0, tiled...  5.97 us
    all_to_all x1, waiting for transfers between devices, local(): lax.all_to_all(block_sum[None], 'ctx', split_axis=2, concat_axis=0, tiled...  4.8 us
    dot_general x2, matrix products, attend_heads(): jnp.einsum('ql,pl->qp', flat_latent, cache_latent[request], preferred_ele...  4.8 us
    dot_general x2, matrix products, attend_heads(): jnp.dot(weights.astype(jnp.bfloat16), cache_latent[request], preferred_el...  4.68 us
  transfers between devices with their start and end apart: 4, of which 3 were waited for; matrix products, arithmetic and copies ran while one was open for 6% of the time, Pallas kernels for 0%

profile of v1, /device:TPU:0, one launch (start us, length us, event | category | flops | bytes accessed | tf_op | source)
XLA Modules:
  0.0 202.3 jit_solution(3345271216129224351)
XLA Ops:
  6.5 0.0 copy-start
  6.5 0.0 copy-start.4
  6.5 1.0 fusion.28
  7.6 1.4 fusion.44
  9.0 0.7 convert_element_type.40
  9.7 1.2 convolution_convert_fusion.3
  10.9 0.0 copy-done
  10.9 1.1 fusion.21
  12.0 0.1 reshape.79
  12.0 23.5 %all_gather.13 = bf16[16,32,64]{2,0,1:T(8,128)(2,1)S(1)} all-gather(bf16[16,2,64]{2,0,1:T(8,128)(2,1)S(1)} %copy.64), channel_id=1, replica_groups=mesh['groups'=2,'ctx'=16] {'ctx'}, dimensions={1}, use_global_device_ids=true | all-gather | bytes 69632 | tf_op jit(solution)/shard_map/all_gather | solution.py:111
  35.6 0.0 copy-done.4
  35.6 0.1 fusion.20
  35.7 18.9 %all_gather.12 = bf16[16,32,512]{2,0,1:T(8,128)(2,1)S(1)} all-gather(bf16[16,2,512]{2,0,1:T(8,128)(2,1)S(1)} %fusion.20), channel_id=1, replica_groups=mesh['groups'=2,'ctx'=16] {'ctx'}, dimensions={1}, use_global_device_ids=true | all-gather | bytes 557056 | tf_op jit(solution)/shard_map/all_gather | solution.py:110
  54.6 0.1 copy.75
  54.7 0.1 copy.76
  54.8 1.3 broadcast_add_fusion
  56.1 0.0 copy-start.2
  56.2 2.4 %fusion.6 = f32[256,2048]{1,0:T(8,128)S(1)} fusion(bf16[256,512]{1,0:T(8,128)(2,1)S(1)} %bitcast.83, bf16[2,2048,512]{2,1,0:T(8,128)(2,1)} %param.17), kind=kOutput, calls=%fused_computation.10 | convolution fusion | flops 536870912 | bytes 4456448 | tf_op jit(solution)/shard_map/ql,pl->qp/dot_general | solution.py:31
  58.6 0.0 copy-done.2
  58.6 0.6 fusion.46
  59.2 0.1 reshape.84
  59.3 0.0 copy-start.3
  59.3 2.4 %fusion.10 = f32[256,2048]{1,0:T(8,128)S(1)} fusion(bf16[256,512]{1,0:T(8,128)(2,1)S(1)} %bitcast.82, bf16[2,2048,512]{2,1,0:T(8,128)(2,1)} %param.17), kind=kOutput, calls=%fused_computation.14 | convolution fusion | flops 536870912 | bytes 4456448 | tf_op jit(solution)/shard_map/ql,pl->qp/dot_general | solution.py:31
  61.7 0.0 copy-done.3
  61.7 1.9 fusion.45
  63.6 0.1 reshape.83
  63.7 0.7 copy.70
  64.4 3.5 %all-to-all-start.1 = ((f32[1,16,32]{1,0,2:T(1,128)}), f32[1,16,32]{1,0,2:T(1,128)S(1)}, u32[]{:S(2)}, u32[]{:S(2)}) async-start(f32[1,16,32]{1,0,2:T(1,128)} %copy.70), calls=%async_computation.1 | async-start | bytes 32768 | tf_op jit(solution)/shard_map/all_to_all | solution.py:117
  67.9 3.8 %fusion.16 = (f32[256]{0:T(256)S(1)}, f32[256]{0:T(256)S(1)}, bf16[256,2048]{1,0:T(8,128)(2,1)}, bf16[256,2048]{1,0:T(8,128)(2,1)}) fusion(f32[256,2048]{1,0:T(8,128)} %get-tuple-element.18, f32[256]{0:T(256)S(1)} %get-tuple-element.17, s32[2048]{0:T(1024)S(1)} %iota_add_fusion, s32[256]{0:T(256)S(1)} %get-tuple-element.22, ...), kind=kLoop, calls=%fused_computation.20 | loop fusion | flops 5242368 | bytes 6305792 | tf_op jit(solution)/shard_map/reduce_sum | solution.py:45
  71.7 0.1 reshape.85
  71.8 0.1 reshape.86
  71.8 0.0 copy-start.1
  71.9 2.8 %fusion.4 = f32[8,32,512]{2,1,0:T(8,128)S(1)} fusion(bf16[8,32,2048]{2,1,0:T(8,128)(2,1)} %bitcast.81, bf16[2,2048,512]{2,1,0:T(8,128)(2,1)} %param.17), kind=kOutput, calls=%fused_computation.8 | convolution fusion | flops 536870912 | bytes 3670016 | tf_op jit(solution)/shard_map/dot_general | solution.py:46
  74.6 0.4 copy-done.1
  75.0 1.9 fusion.8
  76.9 0.7 copy.72
  77.6 0.0 all-to-all-done.1
  77.6 6.0 %all-to-all-start.2 = ((f32[1,16,32]{1,0,2:T(1,128)}), f32[1,16,32]{1,0,2:T(1,128)S(1)}, u32[]{:S(2)}, u32[]{:S(2)}) async-start(f32[1,16,32]{1,0,2:T(1,128)} %copy.72), calls=%async_computation.2 | async-start | bytes 32768 | tf_op jit(solution)/shard_map/all_to_all | solution.py:118
  83.6 0.1 maximum_bitcast_fusion
  83.7 1.6 copy.68
  85.3 0.0 copy-start.5
  85.3 4.8 %all-to-all-done.2 = f32[1,16,32]{1,0,2:T(1,128)S(1)} async-done(((f32[1,16,32]{1,0,2:T(1,128)}), f32[1,16,32]{1,0,2:T(1,128)S(1)}, u32[]{:S(2)}, u32[]{:S(2)}) %all-to-all-start.2) | async-done | bytes 2080 | tf_op jit(solution)/shard_map/all_to_all | solution.py:118
  90.1 3.7 %all-to-all-start = ((f32[1,16,32,512]{3,1,0,2:T(8,128)}), f32[1,16,32,512]{3,1,0,2:T(8,128)S(1)}, u32[]{:S(2)}, u32[]{:S(2)}) async-start(f32[1,16,32,512]{3,1,0,2:T(8,128)} %copy.68), calls=%async_computation | async-start | bytes 2097152 | tf_op jit(solution)/shard_map/all_to_all | solution.py:116
  93.8 0.0 all-gather.3.cloned.1.call-start
  93.9 0.2 copy.71
  94.0 22.6 %all-to-all-done = f32[1,16,32,512]{3,1,0,2:T(8,128)S(1)} async-done(((f32[1,16,32,512]{3,1,0,2:T(8,128)}), f32[1,16,32,512]{3,1,0,2:T(8,128)S(1)}, u32[]{:S(2)}, u32[]{:S(2)}) %all-to-all-start) | async-done | bytes 1048608 | tf_op jit(solution)/shard_map/all_to_all | solution.py:116
  116.6 1.1 fusion.23
  117.7 0.0 copy-done.5
  117.7 0.2 fusion.22
  117.9 3.4 %fusion.36 = f32[16,7168]{1,0:T(8,128)} fusion(bf16[256,7168]{1,0:T(8,128)(2,1)} %param.16, bf16[2,2,8,128]{3,2,1,0:T(8,128)(2,1)S(1)} %fusion.22), kind=kOutput, calls=%fused_computation.48 | convolution fusion | flops 58720256 | bytes 4136960 | tf_op jit(solution)/shard_map/dot_general | solution.py:64
  121.3 0.0 all-gather.3.cloned.1.call-update
  121.3 69.9 %all-gather.3.cloned.1.call-done = f32[256,7168]{1,0:T(8,128)} async-done(((f32[16,7168]{1,0:T(8,128)}), f32[256,7168]{1,0:T(8,128)}) %all-gather.3.cloned.1.call-update) | async-done | bytes 7340048 | tf_op jit(solution)/shard_map/all_gather | solution.py:12
  191.3 4.2 %reduce_sum.59 = bf16[16,7168]{1,0:T(8,128)(2,1)} reduce(f32[16,16,7168]{2,1,0:T(8,128)} %bitcast.78, f32[]{:T(128)} %constant.35.clone.1), dimensions={0}, to_apply=%region_8.9 | reduce | flops 1720320 | bytes 7569412 | tf_op jit(solution)/shard_map/reduce_sum | solution.py:13
  (11 shorter events, 0.2 us)
Async XLA Ops:
  6.5 4.4 %copy-start = (bf16[1536,256]{1,0:T(8,128)(2,1)S(1)}, bf16[1536,256]{1,0:T(8,128)(2,1)}, u32[]{:S(2)}) copy-start(bf16[1536,256]{1,0:T(8,128)(2,1)} %param.12) | copy-start | bytes 2359300
  6.5 29.0 %copy-start.4 = (bf16[2,128,512]{2,1,0:T(8,128)(2,1)S(1)}, bf16[2,128,512]{2,1,0:T(8,128)(2,1)}, u32[]{:S(2)}) copy-start(bf16[2,128,512]{2,1,0:T(8,128)(2,1)} %param.14) | copy-start | bytes 786436
  56.1 2.4 %copy-start.2 = (bf16[2,64,2048]{2,1,0:T(8,128)(2,1)S(1)}, bf16[2,64,2048]{2,1,0:T(8,128)(2,1)}, u32[]{:S(2)}) copy-start(bf16[2,64,2048]{2,1,0:T(8,128)(2,1)} %param.18) | copy-start | bytes 1572868
  59.3 2.4 %copy-start.3 = (bf16[2,64,2048]{2,1,0:T(8,128)(2,1)S(1)}, bf16[2,64,2048]{2,1,0:T(8,128)(2,1)}, u32[]{:S(2)}) copy-start(bf16[2,64,2048]{2,1,0:T(8,128)(2,1)} %param.18) | copy-start | bytes 1572868
  64.4 13.2 %all-to-all-start.1 = ((f32[1,16,32]{1,0,2:T(1,128)}), f32[1,16,32]{1,0,2:T(1,128)S(1)}, u32[]{:S(2)}, u32[]{:S(2)}) async-start(f32[1,16,32]{1,0,2:T(1,128)} %copy.70), calls=%async_computation.1 | async-start | bytes 32768 | tf_op jit(solution)/shard_map/all_to_all | solution.py:117
  71.8 3.1 %copy-start.1 = (bf16[2,2048,512]{2,1,0:T(8,128)(2,1)S(1)}, bf16[2,2048,512]{2,1,0:T(8,128)(2,1)}, u32[]{:S(2)}) copy-start(bf16[2,2048,512]{2,1,0:T(8,128)(2,1)} %param.17) | copy-start | bytes 12582916
  77.6 12.5 %all-to-all-start.2 = ((f32[1,16,32]{1,0,2:T(1,128)}), f32[1,16,32]{1,0,2:T(1,128)S(1)}, u32[]{:S(2)}, u32[]{:S(2)}) async-start(f32[1,16,32]{1,0,2:T(1,128)} %copy.72), calls=%async_computation.2 | async-start | bytes 32768 | tf_op jit(solution)/shard_map/all_to_all | solution.py:118
  85.3 32.4 %copy-start.5 = (bf16[2,512,128]{2,1,0:T(8,128)(2,1)S(1)}, bf16[2,512,128]{2,1,0:T(8,128)(2,1)}, u32[]{:S(2)}) copy-start(bf16[2,512,128]{2,1,0:T(8,128)(2,1)} %param.15) | copy-start | bytes 786436
  90.1 26.5 %all-to-all-start = ((f32[1,16,32,512]{3,1,0,2:T(8,128)}), f32[1,16,32,512]{3,1,0,2:T(8,128)S(1)}, u32[]{:S(2)}, u32[]{:S(2)}) async-start(f32[1,16,32,512]{3,1,0,2:T(8,128)} %copy.68), calls=%async_computation | async-start | bytes 2097152 | tf_op jit(solution)/shard_map/all_to_all | solution.py:116
  93.8 97.5 %all-gather.3.cloned.1.call-start = ((), (), s32[]{:S(2)}) async-start(), calls=%async_computation.3 | async-start | bytes 7798784 | tf_op jit(solution)/shard_map/all_gather | solution.py:12
Sparse Core Ops, SparseCore 0:
  121.5 69.7 all-gather.2
